TPU v7x, 32 devices: a whole 2x2x4 slice. The times are simulated.
32 devices in a mesh: gx: 4 (over y, core), gy: 4 (over z), gz: 2 (over x).
Axes of the slice: x: 2, y: 2, z: 4, core: 2. Of those that a mesh axis runs over, the one named last changes fastest.
Arguments:
- orbital_values: bfloat16 [64, 64, 48, 384], P('gx', 'gy', 'gz'), may hold values from -6 to 6
- dm_slabs: bfloat16 [1536, 8, 384], P(('gx', 'gy', 'gz')), may hold values from -0.015625 to 0.015625
- slab_tile: int32 [1536], P(('gx', 'gy', 'gz')), may hold values from 0 to 15, as said below
- slab_place: int32 [1536], P(('gx', 'gy', 'gz')), may hold values from 0 to 47, as said below
Outputs:
- potential: float32 [64, 64, 48], P('gx', 'gy', 'gz')
- pot_slabs: bfloat16 [1536, 8, 384], P(('gx', 'gy', 'gz'))
Inputs may be any that keep to these rules, and one draw needn't show every extreme that they name: `slab_tile`: within each layer along gz, every tile of that layer has exactly one slab for each place 0 .. 47, held by devices of the same layer; no device holds more than 6 slabs of one tile, and in every layer some device holds exactly 6 slabs of some tile. See slab_tile: the pair (slab_tile, slab_place) is different for all slabs of one layer.
All inputs are finite; a program needn't handle non-finite values.
Results may differ from a plain program's by a relative error of at most 0.0023.
Values may be sent and summed in bfloat16 or wider, within the bound.
No kernel may reach another device: no remote copies, remote signals or barrier semaphores. Data moves between devices by JAX's collectives and lax.ppermute only.
A program may use at most 64 MiB of HBM per device.

v0:
```python
import math

import jax
import jax.numpy as jnp
from jax import lax
from jax.sharding import PartitionSpec as P

RADIUS = 8


ALPHAS = (0.012, 0.025, 0.05, 0.1, 0.2, 0.4, 0.8, 1.6)
MIXES = (0.3, 0.3, 0.32, 0.34, 0.36, 0.38, 0.4, 0.42)


def with_halo(shard, sides, width):
    for axis, dim in sides:
        size, length = (lax.axis_size(axis), shard.shape[dim])
        up = [(i, (i + 1) % size) for i in range(size)]
        down = [(j, i) for i, j in up]
        last = lax.slice_in_dim(shard, length - width, length, axis=dim)
        initial = lax.slice_in_dim(shard, 0, width, axis=dim)
        before = lax.ppermute(last, axis, up)
        after = lax.ppermute(initial, axis, down)
        shard = jnp.concatenate([before, shard, after], axis=dim)
    return shard


def kernel_tables(radius):
    tap_table = [
        [math.exp(-alpha * offset * offset) for offset in range(-radius, radius + 1)]
        for alpha in ALPHAS
    ]
    mix = [
        MIXES[term] / sum((tap * tap for tap in tap_table[term])) ** 1.5
        for term in range(len(ALPHAS))
    ]
    return (tap_table, mix)


def smooth_along(stacked, axis_idx, count, tap_table):
    running = None
    for offset in range(len(tap_table[0])):
        tap_column = jnp.asarray([row[offset] for row in tap_table], dtype=jnp.float32).reshape(
            -1, 1, 1, 1
        )
        addend = tap_column * lax.slice_in_dim(stacked, offset, offset + count, axis=axis_idx)
        running = addend if running is None else running + addend
    return running


def combine_terms(stacked, mix):
    potential = None
    for term_idx in range(stacked.shape[0]):
        addend = mix[term_idx] * stacked[term_idx]
        potential = addend if potential is None else potential + addend
    return potential


def rank_within(key_ids, bucket_ids, is_valid):
    same_bucket = (bucket_ids[:, None] == bucket_ids[None, :]) & is_valid[None, :]
    earlier = key_ids[None, :] < key_ids[:, None]
    return jnp.sum(same_bucket & earlier, axis=1)


def pack_slots(slot_ids, payload, key_ids, slot_count):
    one_hot = slot_ids[:, None] == jnp.arange(slot_count, dtype=jnp.int32)[None, :]
    hot_matrix = one_hot.astype(jnp.bfloat16)
    shipped = jnp.dot(hot_matrix.T, payload, preferred_element_type=jnp.float32).astype(
        jnp.bfloat16
    )
    labels = jnp.sum(jnp.where(one_hot, key_ids[:, None] + 1, 0), axis=0) - 1
    return (hot_matrix, shipped, labels)


def unpack_slots(hot_matrix, arrived):
    return jnp.dot(hot_matrix, arrived, preferred_element_type=jnp.float32).astype(jnp.bfloat16)


def local(orbital_values, dm_slabs, slab_tile, slab_place):
    size_x, size_y, size_z, list_orb = orbital_values.shape
    slab_count, atom_orb, _ = dm_slabs.shape
    list_blk = list_orb // atom_orb
    row_width = atom_orb * list_orb
    across_x = lax.axis_size("gx")
    across_y = lax.axis_size("gy")
    tile_count = across_x * across_y
    capacity = max(2, 2 * ((list_blk + tile_count - 1) // tile_count))
    payload = dm_slabs.reshape(slab_count, row_width)
    key_ids = slab_tile * list_blk + slab_place
    all_valid = jnp.ones((slab_count,), dtype=bool)
    tile_points = size_x * size_y * size_z
    values = orbital_values.reshape(tile_points, list_orb)
    direct_slots = slab_tile * capacity + rank_within(key_ids, slab_tile, all_valid)
    direct_hot, direct_out, direct_keys = pack_slots(
        direct_slots, payload, key_ids, tile_count * capacity
    )
    arrived, arrived_keys = (
        lax.all_to_all(
            direct_out.reshape(tile_count, capacity, row_width),
            ("gx", "gy"),
            split_axis=0,
            concat_axis=0,
            tiled=True,
        ),
        lax.all_to_all(
            direct_keys.reshape(tile_count, capacity),
            ("gx", "gy"),
            split_axis=0,
            concat_axis=0,
            tiled=True,
        ),
    )
    arrived_keys = arrived_keys.reshape(-1)
    places = jnp.where(arrived_keys >= 0, arrived_keys % list_blk, -1)
    place_hot = (places[:, None] == jnp.arange(list_blk, dtype=jnp.int32)[None, :]).astype(
        jnp.bfloat16
    )
    tile_matrix = (
        jnp.dot(place_hot.T, arrived.reshape(-1, row_width), preferred_element_type=jnp.float32)
        .astype(jnp.bfloat16)
        .reshape(list_orb, list_orb)
    )
    product = jnp.dot(values, tile_matrix, preferred_element_type=jnp.float32)
    density = jnp.sum(product * values.astype(jnp.float32), axis=1).reshape(size_x, size_y, size_z)
    tap_table, mix = kernel_tables(RADIUS)
    padded = with_halo(density, (("gx", 0), ("gy", 1), ("gz", 2)), RADIUS)[None]
    stacked = smooth_along(padded, 1, size_x, tap_table)
    stacked = smooth_along(stacked, 2, size_y, tap_table)
    stacked = smooth_along(stacked, 3, size_z, tap_table)
    potential = combine_terms(stacked, mix)
    quad_weight = float(tile_points) ** (-0.5)
    weighted = (
        potential.reshape(tile_points, 1) * values.astype(jnp.float32) * quad_weight
    ).astype(jnp.bfloat16)
    tile_potential = lax.dot_general(
        values, weighted, (((0,), (0,)), ((), ())), preferred_element_type=jnp.float32
    ).astype(jnp.bfloat16)
    pot_rows = tile_potential.reshape(list_blk, row_width)
    returned = jnp.dot(place_hot, pot_rows, preferred_element_type=jnp.float32).astype(jnp.bfloat16)
    back_home = lax.all_to_all(
        returned.reshape(tile_count, capacity, row_width),
        ("gx", "gy"),
        split_axis=0,
        concat_axis=0,
        tiled=True,
    )
    own_rows = unpack_slots(direct_hot, back_home.reshape(-1, row_width))
    return (potential, own_rows.reshape(slab_count, atom_orb, list_orb))


def solution(mesh):
    placed = (
        P("gx", "gy", "gz", None),
        P(("gx", "gy", "gz"), None, None),
        P(("gx", "gy", "gz")),
        P(("gx", "gy", "gz")),
    )
    return jax.shard_map(
        local,
        mesh=mesh,
        in_specs=placed,
        out_specs=(P("gx", "gy", "gz"), P(("gx", "gy", "gz"), None, None)),
        check_vma=False,
    )
```

profile of v0, /device:TPU:0, one launch (start us, length us, event | category | flops | bytes accessed | tf_op | source)
XLA Modules:
  0.0 129.7 jit_solution(13525657361484059463)
XLA Ops:
  0.6 0.7 broadcast_add_fusion.1
  1.3 0.9 convert_reduce_fusion
  2.2 0.7 multiply_add_fusion.2
  2.9 0.1 select_reduce_fusion
  3.0 0.7 sub.7
  3.7 7.4 %all-to-all-start = ((s32[16,1,6]{2,1,0:T(1,128)}), s32[16,1,6]{2,1,0:T(1,128)S(1)}, u32[]{:S(2)}, u32[]{:S(2)}) async-start(s32[16,1,6]{2,1,0:T(1,128)} %bitcast), calls=%async_computation | async-start | bytes 16384 | tf_op jit(solution)/shard_map/all_to_all | solution.py:105
  11.1 1.0 copy.67
  12.1 0.4 convolution_convert_fusion.1
  12.5 1.1 reshape.272
  13.6 3.8 %all-to-all-done = s32[16,1,6]{2,1,0:T(1,128)S(1)} async-done(((s32[16,1,6]{2,1,0:T(1,128)}), s32[16,1,6]{2,1,0:T(1,128)S(1)}, u32[]{:S(2)}, u32[]{:S(2)}) %all-to-all-start) | async-done | bytes 416 | tf_op jit(solution)/shard_map/all_to_all | solution.py:105
  17.4 3.6 %all-to-all-start.1 = ((bf16[16,6,3072]{2,1,0:T(8,128)(2,1)}), bf16[16,6,3072]{2,1,0:T(8,128)(2,1)S(1)}, u32[]{:S(2)}, u32[]{:S(2)}) async-start(bf16[16,6,3072]{2,1,0:T(8,128)(2,1)} %reshape.272), calls=%async_computation.1 | async-start | bytes 1572864 | tf_op jit(solution)/shard_map/all_to_all | solution.py:98
  21.1 6.7 %copy.64 = bf16[6144,384]{0,1:T(8,128)(2,1)} copy(bf16[6144,384]{1,0:T(8,128)(2,1)} %bitcast.65) | data formatting | bytes 9437184 | tf_op jit(solution)/shard_map/reshape | solution.py:92
  27.7 0.1 ge.17
  27.9 0.1 rem.19
  28.0 14.3 %all-to-all-done.1 = bf16[16,6,3072]{2,1,0:T(8,128)(2,1)S(1)} async-done(((bf16[16,6,3072]{2,1,0:T(8,128)(2,1)}), bf16[16,6,3072]{2,1,0:T(8,128)(2,1)S(1)}, u32[]{:S(2)}, u32[]{:S(2)}) %all-to-all-start.1) | async-done | bytes 589856 | tf_op jit(solution)/shard_map/all_to_all | solution.py:98
  42.3 0.2 reshape.273
  42.5 0.4 convolution_convert_fusion.2
  42.8 0.1 reshape.274
  43.0 6.4 %fusion = f32[6144]{0:T(1024)S(1)} fusion(bf16[6144,384]{0,1:T(8,128)(2,1)} %copy.64, bf16[384,384]{1,0:T(8,128)(2,1)S(1)} %reshape.274, bf16[6144,384]{1,0:T(8,128)(2,1)} %bitcast.66), kind=kOutput, calls=%fused_computation.1 | convolution fusion | flops 1819011072 | bytes 9756672 | tf_op jit(solution)/shard_map/dot_general | solution.py:123
  49.4 0.1 slice.218
  49.6 0.1 reshape.276
  49.7 0.1 slice.220
  49.8 1.8 %collective-permute-start.1 = (f32[8,16,24]{2,1,0:T(8,128)S(1)}, f32[8,16,24]{2,1,0:T(8,128)S(1)}, u32[]{:S(2)}, u32[]{:S(2)}) collective-permute-start(f32[8,16,24]{2,1,0:T(8,128)S(1)} %slice.220), channel_id=1, source_target_pairs={{8,0},{16,8},{24,16},{0,24},{9,1},{17,9},{25,17},{1,25},{10,2},{18... | collective-permute-start | bytes 36872 | tf_op jit(solution)/shard_map/ppermute | solution.py:23
  51.6 1.7 %collective-permute-done = f32[8,16,24]{2,1,0:T(8,128)S(1)} collective-permute-done((f32[8,16,24]{2,1,0:T(8,128)S(1)}, f32[8,16,24]{2,1,0:T(8,128)S(1)}, u32[]{:S(2)}, u32[]{:S(2)}) %collective-permute-start) | collective-permute-done | bytes 12320 | tf_op jit(solution)/shard_map/ppermute | solution.py:22
  53.3 0.2 collective-permute-done.1
  53.6 3.8 %collective-permute-start.3 = (f32[32,8,24]{2,1,0:T(8,128)S(1)}, f32[32,8,24]{2,1,0:T(8,128)S(1)}, u32[]{:S(2)}, u32[]{:S(2)}) collective-permute-start(f32[32,8,24]{2,1,0:T(8,128)S(1)} %get-tuple-element.24), channel_id=1, source_target_pairs={{2,0},{4,2},{6,4},{0,6},{3,1},{5,3},{7,5},{1,7},{10,8},{12,10},{14... | collective-permute-start | bytes 73736 | tf_op jit(solution)/shard_map/ppermute | solution.py:23
  57.4 4.4 %collective-permute-done.2 = f32[32,8,24]{2,1,0:T(8,128)S(1)} collective-permute-done((f32[32,8,24]{2,1,0:T(8,128)S(1)}, f32[32,8,24]{2,1,0:T(8,128)S(1)}, u32[]{:S(2)}, u32[]{:S(2)}) %collective-permute-start.2) | collective-permute-done | bytes 24608 | tf_op jit(solution)/shard_map/ppermute | solution.py:22
  61.8 1.0 collective-permute-done.3
  62.9 0.2 fusion.51
  63.1 1.6 %collective-permute-start.4 = (f32[32,32,8]{2,1,0:T(8,128)S(1)}, f32[32,32,8]{2,1,0:T(8,128)S(1)}, u32[]{:S(2)}, u32[]{:S(2)}) collective-permute-start(f32[32,32,8]{2,1,0:T(8,128)S(1)} %get-tuple-element.21), channel_id=1, source_target_pairs={{0,1},{1,0},{2,3},{3,2},{4,5},{5,4},{6,7},{7,6},{8,9},{9,8},{10,11... | collective-permute-start | bytes 98312 | tf_op jit(solution)/shard_map/ppermute | solution.py:22
  64.6 0.5 collective-permute-start.5
  65.2 12.8 %collective-permute-done.4 = f32[32,32,8]{2,1,0:T(8,128)S(1)} collective-permute-done((f32[32,32,8]{2,1,0:T(8,128)S(1)}, f32[32,32,8]{2,1,0:T(8,128)S(1)}, u32[]{:S(2)}, u32[]{:S(2)}) %collective-permute-start.4) | collective-permute-done | bytes 32800 | tf_op jit(solution)/shard_map/ppermute | solution.py:22
  77.9 10.2 %collective-permute-done.5 = f32[32,32,8]{2,1,0:T(8,128)S(1)} collective-permute-done((f32[32,32,8]{2,1,0:T(8,128)S(1)}, f32[32,32,8]{2,1,0:T(8,128)S(1)}, u32[]{:S(2)}, u32[]{:S(2)}) %collective-permute-start.5) | collective-permute-done | bytes 32800 | tf_op jit(solution)/shard_map/ppermute | solution.py:23
  88.1 0.3 maximum_bitcast_fusion
  88.6 0.6 slice_bitcast_fusion.16
  89.2 2.4 %multiply_add_fusion = f32[8,16,32,40]{3,2,1,0:T(8,128)S(1)} fusion(f32[16,32,40]{2,1,0:T(8,128)S(1)} %get-tuple-element.13, f32[16,32,40]{2,1,0:T(8,128)S(1)} %get-tuple-element.5, f32[16,32,40]{2,1,0:T(8,128)S(1)} %get-tuple-element.6, f32[16,32,40]{2,1,0:T(8,128)S(1)} %get-tuple-element.7, f32[16,32,40]{2,1,0:T(8,128)S(1)} %get-tuple-element.8, ...), kind=kLoop, calls=%fused_computation.10 | loop fusion | flops 5242880 | bytes 2048256 | tf_op jit(solution)/shard_map/add | solution.py:47
  91.7 2.2 %fusion.22 = f32[8,16,16,40]{3,2,1,0:T(8,128)S(1)} fusion(f32[8,16,32,40]{3,2,1,0:T(8,128)S(1)} %multiply_add_fusion, f32[8]{0:T(128)S(1)} %copy-done.1, f32[8]{0:T(128)S(1)} %copy-done.2, f32[8]{0:T(128)S(1)} %copy-done.3, f32[8]{0:T(128)S(1)} %copy-done.4, f32[8]{0:T(128)S(1)} %copy-done.5, f32[8]{0:T(128)S(1)} %copy-done.6, f32[8]{0:T(128)S(1)} %copy-done.7, ...), kind=kLoop, calls=%fused_computation.47 | loop fusion | flops 2621440 | bytes 5898496 | tf_op jit(solution)/shard_map/add | solution.py:47
  93.9 4.6 %fusion.7 = f32[8,16,16,24]{3,2,1,0:T(8,128)S(1)} fusion(f32[8,16,16,40]{3,2,1,0:T(8,128)S(1)} %fusion.22, f32[8]{0:T(128)S(1)} %copy-done.1, f32[8]{0:T(128)S(1)} %copy-done.2, f32[8]{0:T(128)S(1)} %copy-done.3, f32[8]{0:T(128)S(1)} %copy-done.4, f32[8]{0:T(128)S(1)} %copy-done.5, f32[8]{0:T(128)S(1)} %copy-done.6, f32[8]{0:T(128)S(1)} %copy-done.7, ...), kind=kLoop, calls=%fused_computation.15 | loop fusion | flops 1572864 | bytes 3539200 | tf_op jit(solution)/shard_map/add | solution.py:47
  98.5 0.1 fusion.38
  98.6 3.9 %fusion.6 = bf16[384,384]{0,1:T(8,128)(2,1)S(1)} fusion(bf16[16,16,24,384]{3,2,1,0:T(8,128)(2,1)S(1)} %bitcast.68, f32[16,16,24]{2,1,0:T(8,128)S(1)} %fusion.38), kind=kOutput, calls=%fused_computation.13 | convolution fusion | flops 1821523968 | bytes 5038080 | tf_op jit(solution)/shard_map/dot_general | solution.py:135
  102.6 0.2 copy.65
  102.8 0.1 reshape.277
  102.9 0.3 convolution_convert_fusion
  103.3 0.2 reshape.278
  103.5 25.0 %all_to_all.16 = bf16[16,6,3072]{2,1,0:T(8,128)(2,1)S(1)} all-to-all(bf16[16,6,3072]{2,1,0:T(8,128)(2,1)S(1)} %reshape.278), channel_id=1, replica_groups=mesh['gx'=4,'gy'=4,'gz'=2] {'gx','gy'}, dimensions={0} | all-to-all | bytes 1179648 | tf_op jit(solution)/shard_map/all_to_all | solution.py:140
  128.5 0.2 reshape.279
  128.7 0.3 convolution_convert_fusion.3
  129.0 0.8 copy.68
  (35 shorter events, 0.4 us)
Async XLA Ops:
  3.7 13.7 %all-to-all-start = ((s32[16,1,6]{2,1,0:T(1,128)}), s32[16,1,6]{2,1,0:T(1,128)S(1)}, u32[]{:S(2)}, u32[]{:S(2)}) async-start(s32[16,1,6]{2,1,0:T(1,128)} %bitcast), calls=%async_computation | async-start | bytes 16384 | tf_op jit(solution)/shard_map/all_to_all | solution.py:105
  17.4 24.8 %all-to-all-start.1 = ((bf16[16,6,3072]{2,1,0:T(8,128)(2,1)}), bf16[16,6,3072]{2,1,0:T(8,128)(2,1)S(1)}, u32[]{:S(2)}, u32[]{:S(2)}) async-start(bf16[16,6,3072]{2,1,0:T(8,128)(2,1)} %reshape.272), calls=%async_computation.1 | async-start | bytes 1572864 | tf_op jit(solution)/shard_map/all_to_all | solution.py:98
  49.5 3.7 %collective-permute-start = (f32[8,16,24]{2,1,0:T(8,128)S(1)}, f32[8,16,24]{2,1,0:T(8,128)S(1)}, u32[]{:S(2)}, u32[]{:S(2)}) collective-permute-start(f32[8,16,24]{2,1,0:T(8,128)S(1)} %slice.218), channel_id=1, source_target_pairs={{0,8},{8,16},{16,24},{24,0},{1,9},{9,17},{17,25},{25,1},{2,10},{10... | collective-permute-start | bytes 36872 | tf_op jit(solution)/shard_map/ppermute | solution.py:22
  49.8 3.7 %collective-permute-start.1 = (f32[8,16,24]{2,1,0:T(8,128)S(1)}, f32[8,16,24]{2,1,0:T(8,128)S(1)}, u32[]{:S(2)}, u32[]{:S(2)}) collective-permute-start(f32[8,16,24]{2,1,0:T(8,128)S(1)} %slice.220), channel_id=1, source_target_pairs={{8,0},{16,8},{24,16},{0,24},{9,1},{17,9},{25,17},{1,25},{10,2},{18... | collective-permute-start | bytes 36872 | tf_op jit(solution)/shard_map/ppermute | solution.py:23
  53.5 8.3 %collective-permute-start.2 = (f32[32,8,24]{2,1,0:T(8,128)S(1)}, f32[32,8,24]{2,1,0:T(8,128)S(1)}, u32[]{:S(2)}, u32[]{:S(2)}) collective-permute-start(f32[32,8,24]{2,1,0:T(8,128)S(1)} %get-tuple-element.23), channel_id=1, source_target_pairs={{0,2},{2,4},{4,6},{6,0},{1,3},{3,5},{5,7},{7,1},{8,10},{10,12},{12... | collective-permute-start | bytes 73736 | tf_op jit(solution)/shard_map/ppermute | solution.py:22
  53.6 9.2 %collective-permute-start.3 = (f32[32,8,24]{2,1,0:T(8,128)S(1)}, f32[32,8,24]{2,1,0:T(8,128)S(1)}, u32[]{:S(2)}, u32[]{:S(2)}) collective-permute-start(f32[32,8,24]{2,1,0:T(8,128)S(1)} %get-tuple-element.24), channel_id=1, source_target_pairs={{2,0},{4,2},{6,4},{0,6},{3,1},{5,3},{7,5},{1,7},{10,8},{12,10},{14... | collective-permute-start | bytes 73736 | tf_op jit(solution)/shard_map/ppermute | solution.py:23
  63.1 14.9 %collective-permute-start.4 = (f32[32,32,8]{2,1,0:T(8,128)S(1)}, f32[32,32,8]{2,1,0:T(8,128)S(1)}, u32[]{:S(2)}, u32[]{:S(2)}) collective-permute-start(f32[32,32,8]{2,1,0:T(8,128)S(1)} %get-tuple-element.21), channel_id=1, source_target_pairs={{0,1},{1,0},{2,3},{3,2},{4,5},{5,4},{6,7},{7,6},{8,9},{9,8},{10,11... | collective-permute-start | bytes 98312 | tf_op jit(solution)/shard_map/ppermute | solution.py:22
  64.6 23.5 %collective-permute-start.5 = (f32[32,32,8]{2,1,0:T(8,128)S(1)}, f32[32,32,8]{2,1,0:T(8,128)S(1)}, u32[]{:S(2)}, u32[]{:S(2)}) collective-permute-start(f32[32,32,8]{2,1,0:T(8,128)S(1)} %get-tuple-element.22), channel_id=1, source_target_pairs={{1,0},{0,1},{3,2},{2,3},{5,4},{4,5},{7,6},{6,7},{9,8},{8,9},{11,10... | collective-permute-start | bytes 98312 | tf_op jit(solution)/shard_map/ppermute | solution.py:23
  88.5 0.7 copy-start.1
  88.5 0.7 copy-start.2
  88.5 0.7 copy-start.3
  88.5 0.7 copy-start.4
  88.5 0.7 copy-start.5
  88.5 0.7 copy-start.6
  88.5 0.7 copy-start.7
  88.5 0.7 copy-start.8
  91.7 6.9 %slice-start = ((s8[4718592]{0:T(1024)(128)(4,1)}), s8[4194304]{0:T(1024)(128)(4,1)S(1)}, s32[]{:S(2)}) async-start(s8[4718592]{0:T(1024)(128)(4,1)} %bitcast.67), calls=%async_computation.3 | async-start | bytes 8388608
  93.9 4.7 %slice-start.1 = ((s8[4718592]{0:T(1024)(128)(4,1)}), s8[524288]{0:T(1024)(128)(4,1)S(1)}, s32[]{:S(2)}) async-start(s8[4718592]{0:T(1024)(128)(4,1)} %bitcast.67), calls=%async_computation.4 | async-start | bytes 1048576
  98.6 3.9 %copy-start = (f32[16,16,24]{2,1,0:T(8,128)}, f32[16,16,24]{2,1,0:T(8,128)S(1)}, u32[]{:S(2)}) copy-start(f32[16,16,24]{2,1,0:T(8,128)S(1)} %fusion.38) | copy-start | bytes 73732
where the time goes:
time: 130 us
  waiting for transfers between devices  48.3 us (37%)
  blocking collectives  25 us (19%)
  starting transfers between devices  18.8 us (14%)
  local copies, waits for them, and re-layouts  12.7 us (10%)
  other arithmetic  12.1 us (9%)
  matrix products  11.7 us (9%)
    all_to_all x1, blocking collectives, local(): lax.all_to_all(returned.reshape(tile_count, capacity, row_width), ('gx',...  25 us
    ppermute x3, waiting for transfers between devices, with_halo(): before = lax.ppermute(last, axis, up)  18.8 us
    all_to_all x1, waiting for transfers between devices, local(): lax.all_to_all(direct_out.reshape(tile_count, capacity, row_width), ('gx'...  14.3 us
    ppermute x3, waiting for transfers between devices, with_halo(): after = lax.ppermute(initial, axis, down)  11.4 us
    add x3, other arithmetic, smooth_along(): running = addend if running is None else running + addend  9.24 us
    all_to_all x1, starting transfers between devices, local(): lax.all_to_all(direct_keys.reshape(tile_count, capacity), ('gx', 'gy'), s...  7.41 us
    reshape x1, local copies, waits for them, and re-layouts, local(): values = orbital_values.reshape(tile_points, list_orb)  6.65 us
    dot_general x1, matrix products, local(): product = jnp.dot(values, tile_matrix, preferred_element_type=jnp.float32)  6.44 us
  transfers between devices with their start and end apart: 8, of which 8 were waited for; matrix products, arithmetic and copies ran while one was open for 7% of the time, Pallas kernels for 0%

commit v1 on v0

v1 whole, which is shorter than its diff:
```python
import functools
import math

import jax
import jax.numpy as jnp
import numpy as np
from jax import lax
from jax.experimental import pallas as pl
from jax.experimental.pallas import tpu as pltpu
from jax.sharding import PartitionSpec as P

RADIUS = 8
LANES = 128

ALPHAS = (0.012, 0.025, 0.05, 0.1, 0.2, 0.4, 0.8, 1.6)
MIXES = (0.3, 0.3, 0.32, 0.34, 0.36, 0.38, 0.4, 0.42)

VMEM_SPEC = pl.BlockSpec(memory_space=pltpu.VMEM)
SMEM_SPEC = pl.BlockSpec(memory_space=pltpu.SMEM)


def kernel_tables(radius):
    tap_table = [
        [math.exp(-alpha * offset * offset) for offset in range(-radius, radius + 1)]
        for alpha in ALPHAS
    ]
    mix = [
        MIXES[term] / sum((tap * tap for tap in tap_table[term])) ** 1.5
        for term in range(len(ALPHAS))
    ]
    return (tap_table, mix)


def for_each_slab(tile_ref, count_ref, tile_count, slab_count, visit):
    for t in range(tile_count):
        count_ref[t] = 0

    def step(i, carry):
        t = tile_ref[i]
        slot = count_ref[t]
        count_ref[t] = slot + 1
        visit(i, t, slot)
        return carry

    lax.fori_loop(0, slab_count, step, 0, unroll=4)


def pack_kernel(capacity, chunks, tile_ref, place_ref, slab_ref, out_ref, count_ref, label_ref):
    tile_count = out_ref.shape[0]
    label_ref[...] = jnp.full(label_ref.shape, -1.0, jnp.float32)

    def visit(i, t, slot):
        slab = slab_ref[i]
        for c in range(chunks):
            out_ref[t, slot * chunks + c] = slab[:, c * LANES : (c + 1) * LANES]
        label = place_ref[i].astype(jnp.float32)
        label_ref[t, pl.ds(slot, 1), :] = jnp.full((1, LANES), label, jnp.float32)

    for_each_slab(tile_ref, count_ref, tile_count, slab_ref.shape[0], visit)
    out_ref[:, capacity * chunks] = label_ref[...].astype(jnp.bfloat16)


def density_kernel(
    capacity, chunks, rows, place_ref, arrived_ref, values_ref, out_ref, wide_ref, turned_ref
):
    tile_count = arrived_ref.shape[0]
    step = pl.program_id(0)
    list_orb = wide_ref.shape[0]

    @pl.when(step == 0)
    def _():
        def visit(j, carry):
            place = place_ref[j]

            @pl.when(place >= 0)
            def _():
                t, k = j // capacity, j % capacity
                row = pl.multiple_of(place * rows, rows)
                for c in range(chunks):
                    wide_ref[pl.ds(row, rows), c * LANES : (c + 1) * LANES] = arrived_ref[
                        t, k * chunks + c
                    ].astype(jnp.float32)

            return carry

        lax.fori_loop(0, tile_count * capacity, visit, 0, unroll=4)
        turned_ref[...] = wide_ref[...].T.astype(jnp.bfloat16)

    planes = values_ref.shape[1] // out_ref.shape[1]
    width = out_ref.shape[1]
    for q in range(planes):
        block = values_ref[:, q * width : (q + 1) * width]
        mixed = jnp.dot(turned_ref[...], block, preferred_element_type=jnp.float32)
        density = jnp.sum(mixed * block.astype(jnp.float32), axis=0, keepdims=True)
        out_ref[pl.ds(step * planes + q, 1), :] = density


def filter_kernel(parts, size_x, size_y, taps_ref, fold_ref, *refs):
    grids, bands = refs[:parts], refs[parts : 2 * parts]
    out_ref, first_ref, second_ref = refs[2 * parts :]
    wide_x, wide_y, size_z = grids[0].shape
    lanes = first_ref.shape[-1]
    total = None
    for grid_ref, band_ref in zip(grids, bands):
        term = jnp.dot(
            grid_ref[...].reshape(wide_x * wide_y, size_z),
            band_ref[...],
            precision=lax.Precision.HIGHEST,
            preferred_element_type=jnp.float32,
        )
        total = term if total is None else total + term
    first_ref[...] = total.reshape(wide_x, wide_y, lanes)

    def tap(distance):
        return jnp.broadcast_to(taps_ref[distance : distance + 1, :], (size_y, lanes))

    def along_y(x, carry):
        run = tap(0) * first_ref[x, RADIUS : RADIUS + size_y, :]
        for d in range(1, RADIUS + 1):
            pair = (
                first_ref[x, RADIUS - d : RADIUS - d + size_y, :]
                + first_ref[x, RADIUS + d : RADIUS + d + size_y, :]
            )
            run = run + tap(d) * pair
        second_ref[x] = run
        return carry

    lax.fori_loop(0, wide_x, along_y, 0)

    def along_x(x, carry):
        run = tap(0) * second_ref[x + RADIUS]
        for d in range(1, RADIUS + 1):
            pair = second_ref[x + (RADIUS - d)] + second_ref[x + (RADIUS + d)]
            run = run + tap(d) * pair
        first_ref[x, 0:size_y, :] = run
        return carry

    lax.fori_loop(0, size_x, along_x, 0)
    filtered = first_ref[0:size_x, 0:size_y, :].reshape(size_x * size_y, lanes)
    folded = jnp.dot(
        filtered,
        fold_ref[...],
        precision=lax.Precision.HIGHEST,
        preferred_element_type=jnp.float32,
    )
    out_ref[...] = folded.reshape(size_x, size_y, size_z)


def potential_kernel(
    capacity, chunks, rows, weight, place_ref, field_ref, values_ref, out_ref, total_ref
):
    step = pl.program_id(0)
    width = field_ref.shape[1]
    planes = values_ref.shape[1] // width
    total = None
    for q in range(planes):
        field = field_ref[pl.ds(step * planes + q, 1), :]
        block = values_ref[:, q * width : (q + 1) * width]
        weighted = (field * block.astype(jnp.float32) * weight).astype(jnp.bfloat16)
        term = lax.dot_general(
            block, weighted, (((1,), (1,)), ((), ())), preferred_element_type=jnp.float32
        )
        total = term if total is None else total + term

    @pl.when(step == 0)
    def _():
        total_ref[...] = total

    @pl.when(step > 0)
    def _():
        total_ref[...] += total

    @pl.when(step == pl.num_programs(0) - 1)
    def _():
        def visit(j, carry):
            t, k = j // capacity, j % capacity
            row = pl.multiple_of(jnp.maximum(place_ref[j], 0) * rows, rows)
            for c in range(chunks):
                out_ref[t, k * chunks + c] = total_ref[
                    pl.ds(row, rows), c * LANES : (c + 1) * LANES
                ].astype(jnp.bfloat16)
            return carry

        lax.fori_loop(0, out_ref.shape[0] * capacity, visit, 0, unroll=4)


def unpack_kernel(chunks, tile_count, tile_ref, back_ref, out_ref, count_ref):
    def visit(i, t, slot):
        for c in range(chunks):
            out_ref[i, :, c * LANES : (c + 1) * LANES] = back_ref[t, slot * chunks + c]

    for_each_slab(tile_ref, count_ref, tile_count, out_ref.shape[0], visit)


def ring(size, shift):
    return [(i, (i + shift) % size) for i in range(size)]


def both_sides(block, axis, dim, width):
    size, length = lax.axis_size(axis), block.shape[dim]
    before = lax.ppermute(
        lax.slice_in_dim(block, length - width, length, axis=dim), axis, ring(size, 1)
    )
    after = lax.ppermute(lax.slice_in_dim(block, 0, width, axis=dim), axis, ring(size, -1))
    return jnp.concatenate([before, block, after], axis=dim)


def band_tables(size_z, neighbours):
    tap_table, mix = kernel_tables(RADIUS)

    def band(shift):
        table = np.zeros((size_z, len(ALPHAS), size_z), np.float64)
        for m in range(len(ALPHAS)):
            for source in range(size_z):
                for target in range(size_z):
                    offset = source + shift - target
                    if abs(offset) <= RADIUS:
                        table[source, m, target] = tap_table[m][offset + RADIUS]
        return table.reshape(size_z, len(ALPHAS) * size_z)

    own, low, high = band(0), band(-size_z), band(size_z)
    bands = {0: [own + low + high], 1: [own, low + high], 2: [own, low, high]}[neighbours]
    taps = np.zeros((16, len(ALPHAS) * size_z), np.float64)
    for d in range(RADIUS + 1):
        taps[d] = np.repeat([row[RADIUS + d] for row in tap_table], size_z)
    fold = np.concatenate([mix[m] * np.eye(size_z) for m in range(len(ALPHAS))], axis=0)
    return (
        [b.astype(np.float32) for b in bands],
        taps.astype(np.float32),
        fold.astype(np.float32),
    )


def local(orbital_values, dm_slabs, slab_tile, slab_place):
    size_x, size_y, size_z, list_orb = orbital_values.shape
    slab_count, atom_orb, _ = dm_slabs.shape
    list_blk = list_orb // atom_orb
    tile_count = lax.axis_size("gx") * lax.axis_size("gy")
    capacity = max(2, 2 * ((list_blk + tile_count - 1) // tile_count))
    chunks = list_orb // LANES
    tile_points = size_x * size_y * size_z
    plane = size_y * size_z
    counts = pltpu.SMEM((tile_count,), jnp.int32)

    packed = pl.pallas_call(
        functools.partial(pack_kernel, capacity, chunks),
        out_shape=jax.ShapeDtypeStruct(
            (tile_count, capacity * chunks + 1, atom_orb, LANES), jnp.bfloat16
        ),
        in_specs=[SMEM_SPEC, SMEM_SPEC, VMEM_SPEC],
        out_specs=VMEM_SPEC,
        scratch_shapes=[counts, pltpu.VMEM((tile_count, atom_orb, LANES), jnp.float32)],
        name="pack",
    )(slab_tile, slab_place, dm_slabs)
    arrived = lax.all_to_all(packed, ("gx", "gy"), split_axis=0, concat_axis=0, tiled=True)
    places = arrived[:, capacity * chunks, :capacity, 0].astype(jnp.int32).reshape(-1)
    turned = orbital_values.reshape(tile_points, list_orb).T

    steps = 4
    slice_spec = pl.BlockSpec((list_orb, tile_points // steps), lambda i: (0, i))
    density = pl.pallas_call(
        functools.partial(density_kernel, capacity, chunks, atom_orb),
        grid=(steps,),
        out_shape=jax.ShapeDtypeStruct((size_x, plane), jnp.float32),
        in_specs=[SMEM_SPEC, VMEM_SPEC, slice_spec],
        out_specs=pl.BlockSpec((size_x, plane), lambda i: (0, 0)),
        scratch_shapes=[
            pltpu.VMEM((list_orb, list_orb), jnp.float32),
            pltpu.VMEM((list_orb, list_orb), jnp.bfloat16),
        ],
        name="density",
    )(places, arrived, turned)

    grid = both_sides(density, "gy", 1, RADIUS * size_z)
    wide_y = grid.shape[1] // size_z
    layers = lax.axis_size("gz")
    if layers == 1:
        stack = grid[None]
    elif layers == 2:
        stack = jnp.stack([grid, lax.ppermute(grid, "gz", ring(layers, 1))])
    else:
        low = lax.ppermute(grid, "gz", ring(layers, 1))
        high = lax.ppermute(grid, "gz", ring(layers, -1))
        stack = jnp.stack([grid, low, high])
    stack = both_sides(stack, "gx", 1, RADIUS)
    parts, wide_x, _ = stack.shape
    stack = stack.reshape(parts, wide_x, wide_y, size_z)
    bands, taps, fold = band_tables(size_z, parts - 1)
    lanes = taps.shape[1]
    potential = pl.pallas_call(
        functools.partial(filter_kernel, parts, size_x, size_y),
        out_shape=jax.ShapeDtypeStruct((size_x, size_y, size_z), jnp.float32),
        in_specs=[VMEM_SPEC] * (2 + 2 * parts),
        out_specs=VMEM_SPEC,
        scratch_shapes=[
            pltpu.VMEM((wide_x, wide_y, lanes), jnp.float32),
            pltpu.VMEM((wide_x, size_y, lanes), jnp.float32),
        ],
        name="filter",
    )(jnp.asarray(taps), jnp.asarray(fold), *[stack[i] for i in range(parts)], *map(jnp.asarray, bands))

    returned = pl.pallas_call(
        functools.partial(
            potential_kernel, capacity, chunks, atom_orb, float(tile_points) ** (-0.5)
        ),
        grid=(steps,),
        out_shape=jax.ShapeDtypeStruct(
            (tile_count, capacity * chunks, atom_orb, LANES), jnp.bfloat16
        ),
        in_specs=[SMEM_SPEC, pl.BlockSpec((size_x, plane), lambda i: (0, 0)), slice_spec],
        out_specs=pl.BlockSpec(
            (tile_count, capacity * chunks, atom_orb, LANES), lambda i: (0, 0, 0, 0)
        ),
        scratch_shapes=[pltpu.VMEM((list_orb, list_orb), jnp.float32)],
        name="potential",
    )(places, potential.reshape(size_x, plane), turned)
    back = lax.all_to_all(returned, ("gx", "gy"), split_axis=0, concat_axis=0, tiled=True)
    own_rows = pl.pallas_call(
        functools.partial(unpack_kernel, chunks, tile_count),
        out_shape=jax.ShapeDtypeStruct((slab_count, atom_orb, list_orb), jnp.bfloat16),
        in_specs=[SMEM_SPEC, VMEM_SPEC],
        out_specs=VMEM_SPEC,
        scratch_shapes=[counts],
        name="unpack",
    )(slab_tile, back)
    return (potential, own_rows)


def solution(mesh):
    placed = (
        P("gx", "gy", "gz", None),
        P(("gx", "gy", "gz"), None, None),
        P(("gx", "gy", "gz")),
        P(("gx", "gy", "gz")),
    )
    return jax.shard_map(
        local,
        mesh=mesh,
        in_specs=placed,
        out_specs=(P("gx", "gy", "gz"), P(("gx", "gy", "gz"), None, None)),
        check_vma=False,
    )
```

time: 130 us -> 95.9 us (0.74)
  waiting for transfers between devices: 48.3 us -> 16.2 us
  Pallas kernels: 0 us -> 25.6 us
  matrix products: 11.7 us -> 0 us
  other arithmetic: 12.1 us -> 1.99 us
  starting transfers between devices: 18.8 us -> 14.6 us
    pallas_call x0 -> x5, Pallas kernels: none -> 25.6 us  [the longest x1 7.81 us: local(): pl.pallas_call(functools.partial(density_kernel, capacity, chunks, atom_o...]
    ppermute x6 -> x5, waiting for transfers between devices: 30.3 us -> 5.27 us  [the longest x2 3.48 us: both_sides(): lax.ppermute(lax.slice_in_dim(block, length - width, length, axis=dim), a...]
    dot_general x6 -> x0, matrix products: 11.7 us -> none  [the longest x1 6.44 us: local(): product = jnp.dot(values, tile_matrix, preferred_element_type=jnp.float32)]
    add x6 -> x0, other arithmetic: 10.7 us -> none  [the longest x3 9.24 us: smooth_along(): running = addend if running is None else running + addend]
    all_to_all x2 -> x1, waiting for transfers between devices: 18.1 us -> 10.9 us  [local(): lax.all_to_all(packed, ('gx', 'gy'), split_axis=0, concat_axis=0, tiled=T...]
    all_to_all x2 -> x1, starting transfers between devices: 11 us -> 7.42 us  [local(): lax.all_to_all(packed, ('gx', 'gy'), split_axis=0, concat_axis=0, tiled=T...]
    squeeze x0 -> x2, local copies, waits for them, and re-layouts: none -> 2.35 us  [local(): stack[i]]
    unnamed x26 -> x2, local copies, waits for them, and re-layouts: 1.89 us -> 0.01 us
  transfers between devices with their start and end apart: 8 -> 6, of which waited for: 8 -> 4; matrix products, arithmetic and copies ran while one was open for 7% -> 8% of each run, Pallas kernels for 0% -> 0%
where the time goes in v1:
time: 95.9 us; the launch traced here: 95 us
  Pallas kernels  25.6 us (27%)
  blocking collectives  23.8 us (25%)
  waiting for transfers between devices  16.2 us (17%)
  starting transfers between devices  14.6 us (15%)
  local copies, waits for them, and re-layouts  12.2 us (13%)
  other arithmetic  1.99 us (2%)
    all_to_all x1, blocking collectives, local(): lax.all_to_all(returned, ('gx', 'gy'), split_axis=0, concat_axis=0, tiled...  23.8 us
    all_to_all x1, waiting for transfers between devices, local(): lax.all_to_all(packed, ('gx', 'gy'), split_axis=0, concat_axis=0, tiled=T...  10.9 us
    pallas_call x1, Pallas kernels, local(): pl.pallas_call(functools.partial(density_kernel, capacity, chunks, atom_o...  7.81 us
    all_to_all x1, starting transfers between devices, local(): lax.all_to_all(packed, ('gx', 'gy'), split_axis=0, concat_axis=0, tiled=T...  7.42 us
    pallas_call x1, Pallas kernels, local(): pl.pallas_call(functools.partial(potential_kernel, capacity, chunks, atom...  7.32 us
    reshape x1, local copies, waits for them, and re-layouts, local(): turned = orbital_values.reshape(tile_points, list_orb).T  6.72 us
    pallas_call x1, Pallas kernels, local(): pl.pallas_call(functools.partial(filter_kernel, parts, size_x, size_y), o...  6.27 us
    ppermute x2, starting transfers between devices, both_sides(): lax.ppermute(lax.slice_in_dim(block, 0, width, axis=dim), axis, ring(size...  5.55 us
  transfers between devices with their start and end apart: 6, of which 4 were waited for; matrix products, arithmetic and copies ran while one was open for 8% of the time, Pallas kernels for 0%

profile of v1, /device:TPU:0, one launch (start us, length us, event | category | flops | bytes accessed | tf_op | source)
XLA Modules:
  0.0 95.0 jit_solution(14207538891357012950)
XLA Ops:
  0.6 2.1 %pack.1 = bf16[16,19,8,128]{3,2,1,0:T(8,128)(2,1)} custom-call(s32[48]{0:T(128)} %tile_ref.3, s32[48]{0:T(128)} %place_ref.1, bf16[48,8,384]{2,1,0:T(8,128)(2,1)} %slab_ref.1), custom_call_target="tpu_custom_call" | custom-call | tf_op jit(solution)/shard_map/pack/pallas_call | solution.py:245
  2.8 7.4 %all-to-all-start = ((bf16[16,19,8,128]{3,2,1,0:T(8,128)(2,1)}), bf16[16,19,8,128]{3,2,1,0:T(8,128)(2,1)S(1)}, u32[]{:S(2)}, u32[]{:S(2)}) async-start(bf16[16,19,8,128]{3,2,1,0:T(8,128)(2,1)} %pack.1), calls=%async_computation | async-start | bytes 1245184 | tf_op jit(solution)/shard_map/all_to_all | solution.py:255
  10.2 6.7 %copy.11 = bf16[6144,384]{0,1:T(8,128)(2,1)} copy(bf16[6144,384]{1,0:T(8,128)(2,1)} %bitcast.7) | data formatting | bytes 9437184 | tf_op jit(solution)/shard_map/reshape | solution.py:257
  16.9 10.9 %all-to-all-done.arrived_ref = bf16[16,19,8,128]{3,2,1,0:T(8,128)(2,1)S(1)} async-done(((bf16[16,19,8,128]{3,2,1,0:T(8,128)(2,1)}), bf16[16,19,8,128]{3,2,1,0:T(8,128)(2,1)S(1)}, u32[]{:S(2)}, u32[]{:S(2)}) %all-to-all-start) | async-done | bytes 622624 | tf_op jit(solution)/shard_map/all_to_all | solution.py:255
  27.9 0.0 copy-start
  27.9 0.3 convert_reduce_fusion
  28.2 0.6 reshape.21.place_ref
  28.8 0.0 copy-done
  28.8 7.8 %density.1 = f32[16,384]{1,0:T(8,128)} custom-call(s32[96]{0:T(128)} %reshape.21.place_ref, bf16[16,19,8,128]{3,2,1,0:T(8,128)(2,1)} %copy-done, bf16[384,6144]{1,0:T(8,128)(2,1)} %bitcast.5), custom_call_target="tpu_custom_call" | custom-call | tf_op jit(solution)/shard_map/density/pallas_call | solution.py:261
  36.6 0.9 fusion.2
  37.5 0.0 collective-permute-start
  37.5 3.8 %collective-permute-start.1 = (f32[16,192]{1,0:T(8,128)S(1)}, f32[16,192]{1,0:T(8,128)S(1)}, u32[]{:S(2)}, u32[]{:S(2)}) collective-permute-start(f32[16,192]{1,0:T(8,128)S(1)} %get-tuple-element.7), channel_id=1, source_target_pairs={{0,6},{2,0},{4,2},{6,4},{1,7},{3,1},{5,3},{7,5},{8,14},{10,8},{12,... | collective-permute-start | bytes 36872 | tf_op jit(solution)/shard_map/ppermute | solution.py:204
  41.3 1.7 %collective-permute-done = f32[16,192]{1,0:T(8,128)S(1)} collective-permute-done((f32[16,192]{1,0:T(8,128)S(1)}, f32[16,192]{1,0:T(8,128)S(1)}, u32[]{:S(2)}, u32[]{:S(2)}) %collective-permute-start) | collective-permute-done | bytes 12320 | tf_op jit(solution)/shard_map/ppermute | solution.py:201
  43.0 0.0 collective-permute-done.1
  43.0 0.8 pad_maximum_fusion.2
  43.9 1.5 %collective-permute-start.2 = (f32[16,768]{1,0:T(8,128)S(1)}, f32[16,768]{1,0:T(8,128)S(1)}, u32[]{:S(2)}, u32[]{:S(2)}) collective-permute-start(f32[16,768]{1,0:T(8,128)S(1)} %pad_maximum_fusion.2), channel_id=1, source_target_pairs={{0,1},{1,0},{2,3},{3,2},{4,5},{5,4},{6,7},{7,6},{8,9},{9,8},{10,11... | collective-permute-start | bytes 147464 | tf_op jit(solution)/shard_map/ppermute | solution.py:280
  45.4 0.8 fusion.3
  46.2 1.8 %collective-permute-done.2 = f32[16,768]{1,0:T(8,128)S(1)} collective-permute-done((f32[16,768]{1,0:T(8,128)S(1)}, f32[16,768]{1,0:T(8,128)S(1)}, u32[]{:S(2)}, u32[]{:S(2)}) %collective-permute-start.2) | collective-permute-done | bytes 49184 | tf_op jit(solution)/shard_map/ppermute | solution.py:280
  48.0 0.1 collective-permute-start.3
  48.1 1.7 %collective-permute-start.4 = (f32[2,8,768]{2,1,0:T(8,128)S(1)}, f32[2,8,768]{2,1,0:T(8,128)S(1)}, u32[]{:S(2)}, u32[]{:S(2)}) collective-permute-start(f32[2,8,768]{2,1,0:T(8,128)S(1)} %get-tuple-element.5), channel_id=1, source_target_pairs={{0,24},{8,0},{16,8},{24,16},{1,25},{9,1},{17,9},{25,17},{2,26},{10... | collective-permute-start | bytes 147464 | tf_op jit(solution)/shard_map/ppermute | solution.py:204
  49.8 1.8 %collective-permute-done.3 = f32[2,8,768]{2,1,0:T(8,128)S(1)} collective-permute-done((f32[2,8,768]{2,1,0:T(8,128)S(1)}, f32[2,8,768]{2,1,0:T(8,128)S(1)}, u32[]{:S(2)}, u32[]{:S(2)}) %collective-permute-start.3) | collective-permute-done | bytes 49184 | tf_op jit(solution)/shard_map/ppermute | solution.py:201
  51.6 0.0 collective-permute-done.4
  51.6 1.2 %squeeze.8.refs_1_ = f32[32,32,24]{2,1,0:T(8,128)} reshape(f32[1,32,768]{2,1,0:T(8,128)S(1)} %get-tuple-element.2) | data formatting | bytes 196608 | tf_op jit(solution)/shard_map/squeeze | solution.py:300
  52.8 1.2 %squeeze.7.refs_0_ = f32[32,32,24]{2,1,0:T(8,128)} reshape(f32[1,32,768]{2,1,0:T(8,128)S(1)} %get-tuple-element.3) | data formatting | bytes 196608 | tf_op jit(solution)/shard_map/squeeze | solution.py:300
  54.0 6.3 %filter.1 = f32[16,16,24]{2,1,0:T(8,128)} custom-call(f32[16,192]{1,0:T(8,128)} %constant.8.clone.taps_ref, f32[192,24]{1,0:T(8,128)} %constant.9.clone.fold_ref, f32[32,32,24]{2,1,0:T(8,128)} %squeeze.7.refs_0_, f32[32,32,24]{2,1,0:T(8,128)} %squeeze.8.refs_1_, f32[24,192]{1,0:T(8,128)} %constant.10.clone.refs_2_, f32[24,192]{1,0:T(8,128)} %constant.11.clone.refs_3_), custom_call_target="tpu_custom_call" | custom-call | tf_op jit(solution)/shard_map/filter/pallas_call | solution.py:290
  60.2 1.6 %reshape.20.field_ref = f32[16,384]{1,0:T(8,128)} reshape(f32[16,16,24]{2,1,0:T(8,128)} %filter.1) | data formatting | bytes 49152 | tf_op jit(solution)/shard_map/reshape | solution.py:316
  61.9 7.3 %potential.1 = bf16[16,18,8,128]{3,2,1,0:T(8,128)(2,1)} custom-call(s32[96]{0:T(128)} %reshape.21.place_ref, f32[16,384]{1,0:T(8,128)} %reshape.20.field_ref, bf16[384,6144]{1,0:T(8,128)(2,1)} %bitcast.6), custom_call_target="tpu_custom_call" | custom-call | tf_op jit(solution)/shard_map/potential/pallas_call | solution.py:302
  69.2 23.8 %all_to_all.10.back_ref = bf16[16,18,8,128]{3,2,1,0:T(8,128)(2,1)} all-to-all(bf16[16,18,8,128]{3,2,1,0:T(8,128)(2,1)} %potential.1), channel_id=1, replica_groups=mesh['gx'=4,'gy'=4,'gz'=2] {'gx','gy'}, dimensions={0} | all-to-all | bytes 1179648 | tf_op jit(solution)/shard_map/all_to_all | solution.py:317
  92.9 2.1 %unpack.1 = bf16[48,8,384]{2,1,0:T(8,128)(2,1)} custom-call(s32[48]{0:T(128)} %tile_ref.3, bf16[16,18,8,128]{3,2,1,0:T(8,128)(2,1)} %all_to_all.10.back_ref), custom_call_target="tpu_custom_call" | custom-call | tf_op jit(solution)/shard_map/unpack/pallas_call | solution.py:318
  (3 shorter events, 0.0 us)
Async XLA Ops:
  2.8 25.1 %all-to-all-start = ((bf16[16,19,8,128]{3,2,1,0:T(8,128)(2,1)}), bf16[16,19,8,128]{3,2,1,0:T(8,128)(2,1)S(1)}, u32[]{:S(2)}, u32[]{:S(2)}) async-start(bf16[16,19,8,128]{3,2,1,0:T(8,128)(2,1)} %pack.1), calls=%async_computation | async-start | bytes 1245184 | tf_op jit(solution)/shard_map/all_to_all | solution.py:255
  27.9 1.0 %copy-start = (bf16[16,19,8,128]{3,2,1,0:T(8,128)(2,1)}, bf16[16,19,8,128]{3,2,1,0:T(8,128)(2,1)S(1)}, u32[]{:S(2)}) copy-start(bf16[16,19,8,128]{3,2,1,0:T(8,128)(2,1)S(1)} %all-to-all-done.arrived_ref) | copy-start | bytes 1867780
  37.5 5.5 %collective-permute-start = (f32[16,192]{1,0:T(8,128)S(1)}, f32[16,192]{1,0:T(8,128)S(1)}, u32[]{:S(2)}, u32[]{:S(2)}) collective-permute-start(f32[16,192]{1,0:T(8,128)S(1)} %get-tuple-element.6), channel_id=1, source_target_pairs={{0,2},{2,4},{4,6},{6,0},{1,3},{3,5},{5,7},{7,1},{8,10},{10,12},{12... | collective-permute-start | bytes 36872 | tf_op jit(solution)/shard_map/ppermute | solution.py:201
  37.5 5.5 %collective-permute-start.1 = (f32[16,192]{1,0:T(8,128)S(1)}, f32[16,192]{1,0:T(8,128)S(1)}, u32[]{:S(2)}, u32[]{:S(2)}) collective-permute-start(f32[16,192]{1,0:T(8,128)S(1)} %get-tuple-element.7), channel_id=1, source_target_pairs={{0,6},{2,0},{4,2},{6,4},{1,7},{3,1},{5,3},{7,5},{8,14},{10,8},{12,... | collective-permute-start | bytes 36872 | tf_op jit(solution)/shard_map/ppermute | solution.py:204
  43.9 4.1 %collective-permute-start.2 = (f32[16,768]{1,0:T(8,128)S(1)}, f32[16,768]{1,0:T(8,128)S(1)}, u32[]{:S(2)}, u32[]{:S(2)}) collective-permute-start(f32[16,768]{1,0:T(8,128)S(1)} %pad_maximum_fusion.2), channel_id=1, source_target_pairs={{0,1},{1,0},{2,3},{3,2},{4,5},{5,4},{6,7},{7,6},{8,9},{9,8},{10,11... | collective-permute-start | bytes 147464 | tf_op jit(solution)/shard_map/ppermute | solution.py:280
  48.0 3.6 %collective-permute-start.3 = (f32[2,8,768]{2,1,0:T(8,128)S(1)}, f32[2,8,768]{2,1,0:T(8,128)S(1)}, u32[]{:S(2)}, u32[]{:S(2)}) collective-permute-start(f32[2,8,768]{2,1,0:T(8,128)S(1)} %get-tuple-element.4), channel_id=1, source_target_pairs={{0,8},{8,16},{16,24},{24,0},{1,9},{9,17},{17,25},{25,1},{2,10},{10... | collective-permute-start | bytes 147464 | tf_op jit(solution)/shard_map/ppermute | solution.py:201
  48.1 3.5 %collective-permute-start.4 = (f32[2,8,768]{2,1,0:T(8,128)S(1)}, f32[2,8,768]{2,1,0:T(8,128)S(1)}, u32[]{:S(2)}, u32[]{:S(2)}) collective-permute-start(f32[2,8,768]{2,1,0:T(8,128)S(1)} %get-tuple-element.5), channel_id=1, source_target_pairs={{0,24},{8,0},{16,8},{24,16},{1,25},{9,1},{17,9},{25,17},{2,26},{10... | collective-permute-start | bytes 147464 | tf_op jit(solution)/shard_map/ppermute | solution.py:204
